TPU v7x, 256 devices: a whole 4x4x8 slice. The times are simulated.
256 devices in a mesh: tm: 64 (over y, z_lo, x, core), floor: 4 (over z_hi).
Axes of the slice: x: 4, y: 4, z: 8 (z_hi: 4, z_lo: 2; z = z_hi * 2 + z_lo), core: 2. Of those that a mesh axis runs over, the one named last changes fastest.
Arguments:
- samples: bfloat16 [64, 16, 32768], P('tm', None, 'floor'), may hold values from -6 to 6
- operator: bfloat16 [64, 512, 32768], P('tm', None, 'floor'), may hold values from -0.00390625 to 0.00390625
Outputs:
- sensor_data: bfloat16 [64, 16, 512], P('tm', None, 'floor')
All inputs are finite; a program needn't handle non-finite values.
Results may differ from a plain program's by a relative error of at most 0.0013.
Values may be sent and summed in bfloat16 or wider, within the bound.
No kernel may reach another device: no remote copies, remote signals or barrier semaphores. Data moves between devices by JAX's collectives and lax.ppermute only.
A program may use at most 64 MiB of HBM per device.

v0:
```python
import jax
import jax.numpy as jnp
from jax import lax
from jax.sharding import PartitionSpec as P


def local(samples, operator):
    lag = lax.axis_index("tm")
    blocks = lax.axis_size("tm")
    kernel = operator[0]
    images = jnp.einsum(
        "cki,si->cks",
        lax.all_gather(samples, "tm", axis=0, tiled=True),
        kernel,
        preferred_element_type=jnp.float32,
    )
    padded = jnp.pad(images, ((blocks, 0), (0, 0), (0, 0)))
    shifted = lax.dynamic_slice_in_dim(padded, blocks - lag, blocks, 0)
    mine = lax.all_to_all(shifted, "tm", 0, 0, tiled=True).sum(0)
    parts = mine.reshape(mine.shape[0], lax.axis_size("floor"), -1).swapaxes(0, 1)
    records = lax.all_to_all(parts, "floor", 0, 0, tiled=True).sum(0)
    return records[None].astype(jnp.bfloat16)


def solution(mesh):
    placed = (P("tm", None, "floor"), P("tm", None, "floor"))
    return jax.shard_map(
        local, mesh=mesh, in_specs=placed, out_specs=P("tm", None, "floor"), check_vma=False
    )
```

profile of v0, /device:TPU:1, one launch (start us, length us, event | category | flops | bytes accessed | tf_op | source)
XLA Modules:
  0.0 216.1 jit_solution(414119215055207284)
XLA Ops:
  6.5 0.0 all-gather.2.cloned.1.call-start
  6.5 0.7 all-gather.2.cloned.1.call-update
  7.3 131.9 %all-gather.2.cloned.1.call-done = bf16[64,16,8192]{2,1,0:T(8,128)(2,1)} async-done(((bf16[1,16,8192]{2,1,0:T(8,128)(2,1)}), bf16[64,16,8192]{2,1,0:T(8,128)(2,1)}) %all-gather.2.cloned.1.call-update) | async-done | bytes 16777232 | tf_op jit(solution)/shard_map/all_gather | solution.py:13
  139.1 21.5 %fusion = f32[128,16,512]{2,1,0:T(8,128)S(1)} fusion(bf16[64,16,8192]{2,1,0:T(8,128)(2,1)} %all-gather.2.cloned.1.call-done, bf16[1,512,8192]{2,1,0:T(8,128)(2,1)} %param.3), kind=kOutput, calls=%fused_computation | convolution fusion | flops 8589934592 | bytes 29360128 | tf_op jit(solution)/shard_map/jit(_pad)/pad | solution.py:17
  160.7 0.2 constant_dynamic-slice_fusion
  160.9 35.0 %all_to_all.10 = f32[64,16,512]{2,1,0:T(8,128)S(1)} all-to-all(f32[64,16,512]{2,1,0:T(8,128)S(1)} %constant_dynamic-slice_fusion), channel_id=1, replica_groups=mesh['tm'=64,'floor'=4] {'tm'}, dimensions={0} | all-to-all | bytes 4194304 | tf_op jit(solution)/shard_map/all_to_all | solution.py:19
  195.9 0.1 reduce_sum.18
  196.1 12.6 %all_to_all.11 = f32[4,16,128]{2,1,0:T(8,128)S(1)} all-to-all(f32[4,16,128]{2,1,0:T(8,128)S(1)} %copy.3), channel_id=1, replica_groups=mesh['tm'=64,'floor'=4] {'floor'}, dimensions={0} | all-to-all | bytes 65536 | tf_op jit(solution)/shard_map/all_to_all | solution.py:21
  208.7 0.6 reduce_sum.19
  (2 shorter events, 0.0 us)
Async XLA Ops:
  6.5 132.6 %all-gather.2.cloned.1.call-start = ((), (), s32[]{:S(2)}) async-start(), calls=%async_computation.2 | async-start | bytes 17039360 | tf_op jit(solution)/shard_map/all_gather | solution.py:13
Sparse Core Ops, SparseCore 0:
  9.2 129.8 all-gather.1
where the time goes:
time: 216 us
  waiting for transfers between devices  133 us (62%)
  blocking collectives  47.6 us (22%)
  matrix products  21.5 us (10%)
  between operations  13.4 us (6%)
    all_gather x1, waiting for transfers between devices, local(): lax.all_gather(samples, 'tm', axis=0, tiled=True)  132 us
    all_to_all x1, blocking collectives, local(): mine = lax.all_to_all(shifted, 'tm', 0, 0, tiled=True).sum(0)  35 us
    pad x1, matrix products, local(): padded = jnp.pad(images, ((blocks, 0), (0, 0), (0, 0)))  21.5 us
    all_to_all x1, blocking collectives, local(): records = lax.all_to_all(parts, 'floor', 0, 0, tiled=True).sum(0)  12.6 us
  transfers between devices with their start and end apart: 1, of which 1 were waited for; matrix products, arithmetic and copies ran while one was open for 0% of the time, Pallas kernels for 0%

commit v1 on v0

--- a/solution.py
+++ b/solution.py
@@ -2,6 +2,11 @@
 import jax.numpy as jnp
 from jax import lax
 from jax.sharding import PartitionSpec as P
+
+
+def exchange_gather(x, axis, dim):
+    outgoing = jnp.stack([x] * lax.axis_size(axis))
+    return jnp.concatenate(lax.all_to_all(outgoing, axis, 0, 0), axis=dim)
 
 
 def local(samples, operator):
@@ -9,10 +14,7 @@
     blocks = lax.axis_size("tm")
     kernel = operator[0]
     images = jnp.einsum(
-        "cki,si->cks",
-        lax.all_gather(samples, "tm", axis=0, tiled=True),
-        kernel,
-        preferred_element_type=jnp.float32,
+        "cki,si->cks", exchange_gather(samples, "tm", 0), kernel, preferred_element_type=jnp.float32
     )
     padded = jnp.pad(images, ((blocks, 0), (0, 0), (0, 0)))
     shifted = lax.dynamic_slice_in_dim(padded, blocks - lag, blocks, 0)

time: 216 us -> 327 us (1.51)
  waiting for transfers between devices: 133 us -> 237 us
  between operations: 13.4 us -> 0.05 us
  starting transfers between devices: 0.01 us -> 10.5 us
  local copies, waits for them, and re-layouts: 0.21 us -> 6.89 us
    all_to_all x0 -> x1, waiting for transfers between devices: none -> 237 us  [exchange_gather(): return jnp.concatenate(lax.all_to_all(outgoing, axis, 0, 0), axis=dim)]
    all_gather x1 -> x0, waiting for transfers between devices: 132 us -> none  [local(): lax.all_gather(samples, 'tm', axis=0, tiled=True)]
    all_to_all x0 -> x1, starting transfers between devices: none -> 10.5 us  [exchange_gather(): return jnp.concatenate(lax.all_to_all(outgoing, axis, 0, 0), axis=dim)]
    another operation x0 -> x1, local copies, waits for them, and re-layouts: none -> 6.68 us  [exchange_gather(): outgoing = jnp.stack([x] * lax.axis_size(axis))]
where the time goes in v1:
time: 327 us
  waiting for transfers between devices  237 us (72%)
  blocking collectives  49.7 us (15%)
  matrix products  21.5 us (7%)
  starting transfers between devices  10.5 us (3%)
  local copies, waits for them, and re-layouts  6.89 us (2%)
    all_to_all x1, waiting for transfers between devices, exchange_gather(): return jnp.concatenate(lax.all_to_all(outgoing, axis, 0, 0), axis=dim)  237 us
    all_to_all x1, blocking collectives, local(): mine = lax.all_to_all(shifted, 'tm', 0, 0, tiled=True).sum(0)  35.9 us
    pad x1, matrix products, local(): padded = jnp.pad(images, ((blocks, 0), (0, 0), (0, 0)))  21.5 us
    all_to_all x1, blocking collectives, local(): records = lax.all_to_all(parts, 'floor', 0, 0, tiled=True).sum(0)  13.8 us
    all_to_all x1, starting transfers between devices, exchange_gather(): return jnp.concatenate(lax.all_to_all(outgoing, axis, 0, 0), axis=dim)  10.5 us
    another operation x1, local copies, waits for them, and re-layouts, exchange_gather(): outgoing = jnp.stack([x] * lax.axis_size(axis))  6.68 us
  transfers between devices with their start and end apart: 1, of which 1 were waited for; matrix products, arithmetic and copies ran while one was open for 0% of the time, Pallas kernels for 0%

profile of v1, /device:TPU:1, one launch (start us, length us, event | category | flops | bytes accessed | tf_op | source)
XLA Modules:
  0.0 326.6 jit_solution(758732552583135287)
XLA Ops:
  0.0 6.7 %stack.2 = bf16[64,1,16,8192]{3,2,1,0:T(8,128)(2,1)} broadcast(bf16[16,8192]{1,0:T(8,128)(2,1)} %bitcast.12), dimensions={2,3} | broadcast | bytes 17039360 | tf_op jit(solution)/shard_map/stack | solution.py:8
  6.7 10.5 %all-to-all-start = ((bf16[64,1,16,8192]{3,2,1,0:T(8,128)(2,1)}), bf16[64,1,16,8192]{3,2,1,0:T(8,128)(2,1)}, u32[]{:S(2)}, u32[]{:S(2)}) async-start(bf16[64,1,16,8192]{3,2,1,0:T(8,128)(2,1)} %stack.2), calls=%async_computation | async-start | bytes 33554432 | tf_op jit(solution)/shard_map/all_to_all | solution.py:9
  17.2 237.2 %all-to-all-done = bf16[64,1,16,8192]{3,2,1,0:T(8,128)(2,1)} async-done(((bf16[64,1,16,8192]{3,2,1,0:T(8,128)(2,1)}), bf16[64,1,16,8192]{3,2,1,0:T(8,128)(2,1)}, u32[]{:S(2)}, u32[]{:S(2)}) %all-to-all-start) | async-done | bytes 16777248 | tf_op jit(solution)/shard_map/all_to_all | solution.py:9
  254.4 21.5 %fusion = f32[128,16,512]{2,1,0:T(8,128)S(1)} fusion(bf16[64,1,16,8192]{3,2,1,0:T(8,128)(2,1)} %all-to-all-done, bf16[1,512,8192]{2,1,0:T(8,128)(2,1)} %param.3), kind=kOutput, calls=%fused_computation | convolution fusion | flops 8589934592 | bytes 29360128 | tf_op jit(solution)/shard_map/jit(_pad)/pad | solution.py:19
  275.9 0.2 constant_dynamic-slice_fusion
  276.1 35.9 %all_to_all.15 = f32[64,16,512]{2,1,0:T(8,128)S(1)} all-to-all(f32[64,16,512]{2,1,0:T(8,128)S(1)} %constant_dynamic-slice_fusion), channel_id=1, replica_groups=mesh['tm'=64,'floor'=4] {'tm'}, dimensions={0} | all-to-all | bytes 4194304 | tf_op jit(solution)/shard_map/all_to_all | solution.py:21
  312.0 0.1 reduce_sum.18
  312.2 13.8 %all_to_all.16 = f32[4,16,128]{2,1,0:T(8,128)S(1)} all-to-all(f32[4,16,128]{2,1,0:T(8,128)S(1)} %copy.3), channel_id=1, replica_groups=mesh['tm'=64,'floor'=4] {'floor'}, dimensions={0} | all-to-all | bytes 65536 | tf_op jit(solution)/shard_map/all_to_all | solution.py:23
  326.0 0.6 reduce_sum.19
  (2 shorter events, 0.0 us)
Async XLA Ops:
  6.7 247.7 %all-to-all-start = ((bf16[64,1,16,8192]{3,2,1,0:T(8,128)(2,1)}), bf16[64,1,16,8192]{3,2,1,0:T(8,128)(2,1)}, u32[]{:S(2)}, u32[]{:S(2)}) async-start(bf16[64,1,16,8192]{3,2,1,0:T(8,128)(2,1)} %stack.2), calls=%async_computation | async-start | bytes 33554432 | tf_op jit(solution)/shard_map/all_to_all | solution.py:9
